TPU v7x, 256 devices: a whole 4x4x8 slice. The times are simulated.
256 devices in a mesh: seq: 128 (over x_lo, y, z, core), ch: 2 (over x_hi).
Axes of the slice: x: 4 (x_hi: 2, x_lo: 2; x = x_hi * 2 + x_lo), y: 4, z: 8, core: 2. Of those that a mesh axis runs over, the one named last changes fastest.
Arguments:
- query_input: bfloat16 [16384, 1024], P('seq', 'ch'), may hold values from -6 to 6
- key_input: bfloat16 [16384, 1024], P('seq', 'ch'), may hold values from -6 to 6
- value_input: bfloat16 [16384, 1024], P('seq', 'ch'), may hold values from -6 to 6
- short_kernel: float32 [3, 7, 1024], P(None, None, 'ch'), may hold values from -2 to 2
- residues: float32 [16, 1024], P(None, 'ch'), may hold values from -1.5 to 1.5
- rates: float32 [16, 1024], P(None, 'ch'), may hold values from 3.0517578e-05 to 0.03
- out_weight: bfloat16 [1024, 8192], P('ch'), may hold values from -0.1875 to 0.1875
Outputs:
- mixed: float32 [16384, 8192], P(('seq', 'ch'))
All inputs are finite; a program needn't handle non-finite values.
Results may differ from a plain program's by a relative error of at most 0.015.
Values may be sent and summed in bfloat16 or wider, within the bound.
A program may use at most 64 MiB of HBM per device.

v0:
```python
import functools
import math

import jax
import jax.numpy as jnp
from jax import lax
from jax.experimental import pallas as pl
from jax.experimental.pallas import tpu as pltpu
from jax.sharding import PartitionSpec as P

SEQ_FACTORS = (2, 4, 8, 2)
MESH = pl.DeviceIdType.MESH
BLOCK = 8
TAIL = 16


def scan_kernel(
    query_hbm,
    key_hbm,
    value_hbm,
    short_ref,
    residue_ref,
    rate_ref,
    gated_ref,
    raw,
    ext,
    tails,
    query_buf,
    driven,
    local_states,
    entry_states,
    state_rows,
    powers,
    response,
    taps,
    own_total,
    pair_total,
    ring_in,
    ring_total,
    plane_in,
    carry_half,
    carry_in,
    load_sem,
    tail_send,
    tail_recv,
    pair_send,
    pair_recv,
    ring_send,
    ring_recv,
    plane_send,
    plane_recv,
    half_send,
    half_recv,
):
    nx, ny, nz, nc = SEQ_FACTORS
    planes = nx * ny
    devices = planes * nz * nc
    tokens, width = query_buf.shape
    half = width // 2
    blocks = tokens // BLOCK
    me = lax.axis_index("seq")
    ch = lax.axis_index("ch")
    core = lax.rem(me, nc)
    chip = lax.div(me, nc)
    z = lax.rem(chip, nz)
    plane = lax.div(chip, nz)
    after = lax.rem(me + 1, devices)
    before = lax.rem(me + devices - 1, devices)
    sibling = chip * nc + (1 - core)

    loads = []
    for at, source in enumerate((key_hbm, value_hbm, query_hbm)):
        copy = pltpu.make_async_copy(source, raw.at[at], load_sem.at[at])
        copy.start()
        loads.append(copy)

    ring_peers = []
    for step in range(1, nz):
        ring_peers.append((plane * nz + lax.rem(z + step, nz)) * nc + core)
    plane_peers = []
    for step in range(1, planes):
        plane_peers.append((lax.rem(plane + step, planes) * nz + z) * nc + core)
    peers = [after, before, sibling] + ring_peers + plane_peers
    barrier = pltpu.get_barrier_semaphore()
    for peer in peers:
        pl.semaphore_signal(barrier, inc=1, device_id=(peer, ch), device_id_type=MESH)

    for part in range(2):
        columns = slice(part * half, (part + 1) * half)
        decay = jnp.exp(-rate_ref[:, columns])
        power = jnp.ones_like(decay)
        scaled = residue_ref[:, columns] * jnp.sqrt(2.0 * rate_ref[:, columns])
        for n in range(BLOCK):
            powers[n, part] = power
            tap = jnp.sum(scaled * power, axis=0, keepdims=True)
            rows = lax.broadcasted_iota(jnp.int32, (BLOCK, half), 0)
            taps[n, part] = jnp.where(rows >= n, jnp.broadcast_to(tap, (BLOCK, half)), 0.0)
            power = power * decay
        powers[BLOCK, part] = power
    ages = lax.broadcasted_iota(jnp.int32, (BLOCK, width), 0).astype(jnp.float32) + 1.0
    order = rate_ref.shape[0]
    for r in range(order):
        rate_row = rate_ref[r : r + 1, :]
        scale_row = residue_ref[r : r + 1, :] * jnp.sqrt(2.0 * rate_row)
        response[r] = scale_row * jnp.exp(-(ages * rate_row))

    pl.semaphore_wait(barrier, len(peers))
    for copy in loads:
        copy.wait()
    tail_copies = []
    for at, source in enumerate((key_hbm, value_hbm, query_hbm)):
        copy = pltpu.make_async_remote_copy(
            src_ref=source.at[pl.ds(tokens - TAIL, TAIL)],
            dst_ref=tails.at[at],
            send_sem=tail_send.at[at],
            recv_sem=tail_recv.at[at],
            device_id=(after, ch),
            device_id_type=MESH,
        )
        copy.start()
        tail_copies.append(copy)
    for copy in tail_copies:
        copy.wait_recv()
    for at in range(3):
        last = tails[at].astype(jnp.float32)[TAIL - BLOCK :]
        ext[at, 0:BLOCK] = jnp.where(me == 0, 0.0, last)
        ext[at, BLOCK:] = raw[at].astype(jnp.float32)

    def short_rows(at, filter_at, start):
        window = ext[at, pl.ds(start, 2 * BLOCK + BLOCK)]
        total = short_ref[filter_at, 0:1, :] * window[BLOCK:]
        for j in range(1, short_ref.shape[1]):
            total = total + short_ref[filter_at, j : j + 1, :] * window[BLOCK - j : 3 * BLOCK - j]
        return total

    @pl.loop(0, tokens // (2 * BLOCK))
    def _(i):
        start = pl.multiple_of(i * (2 * BLOCK), 2 * BLOCK)
        driven[pl.ds(start, 2 * BLOCK)] = short_rows(0, 1, start) * short_rows(1, 2, start)

    for part in range(2):
        columns = slice(part * half, (part + 1) * half)

        def advance(b, state):
            local_states[b, part] = state
            rows = driven[pl.ds(pl.multiple_of(b * BLOCK, BLOCK), BLOCK), columns]
            state = state * powers[BLOCK, part]
            for j in range(BLOCK):
                state = state + powers[BLOCK - 1 - j, part] * rows[j : j + 1, :]
            return state

        own_total[part] = lax.fori_loop(0, blocks, advance, jnp.zeros((order, half), jnp.float32))

    pair_copy = pltpu.make_async_remote_copy(
        src_ref=own_total,
        dst_ref=pair_total,
        send_sem=pair_send,
        recv_sem=pair_recv,
        device_id=(sibling, ch),
        device_id_type=MESH,
    )
    pair_copy.start()

    @pl.loop(0, tokens // (2 * BLOCK))
    def _(i):
        start = pl.multiple_of(i * (2 * BLOCK), 2 * BLOCK)
        query_buf[pl.ds(start, 2 * BLOCK)] = short_rows(2, 0, start).astype(query_buf.dtype)

    pair_copy.wait_recv()
    my_rates = jnp.where(core == 0, rate_ref[:, 0:half], rate_ref[:, half:])
    mine = own_total[core]
    theirs = pair_total[core]
    first = jnp.where(core == 0, mine, theirs)
    second = jnp.where(core == 0, theirs, mine)
    step_decay = jnp.exp(-(my_rates * float(tokens)))
    ring_in[z] = first * step_decay + second

    ring_copies = []
    for at, peer in enumerate(ring_peers):
        copy = pltpu.make_async_remote_copy(
            src_ref=ring_in.at[z],
            dst_ref=ring_in.at[z],
            send_sem=ring_send.at[at],
            recv_sem=ring_recv.at[at],
            device_id=(peer, ch),
            device_id_type=MESH,
        )
        copy.start()
        ring_copies.append(copy)
    for copy in ring_copies:
        copy.wait_recv()
    chip_decay = jnp.exp(-(my_rates * float(tokens * nc)))
    total = jnp.zeros((order, half), jnp.float32)
    before_me = total
    for at in range(nz):
        before_me = jnp.where(at == z, total, before_me)
        total = total * chip_decay + ring_in[at]
    plane_in[plane] = total

    plane_copies = []
    for at, peer in enumerate(plane_peers):
        copy = pltpu.make_async_remote_copy(
            src_ref=plane_in.at[plane],
            dst_ref=plane_in.at[plane],
            send_sem=plane_send.at[at],
            recv_sem=plane_recv.at[at],
            device_id=(peer, ch),
            device_id_type=MESH,
        )
        copy.start()
        plane_copies.append(copy)
    for copy in plane_copies:
        copy.wait_recv()
    row_decay = jnp.exp(-(my_rates * float(tokens * nc * nz)))
    total = jnp.zeros((order, half), jnp.float32)
    earlier = total
    for at in range(planes):
        earlier = jnp.where(at == plane, total, earlier)
        total = total * row_decay + plane_in[at]
    distance = (z * (tokens * nc)).astype(jnp.float32)
    carry_half[...] = before_me + earlier * jnp.exp(-(my_rates * distance))

    half_copy = pltpu.make_async_remote_copy(
        src_ref=carry_half,
        dst_ref=carry_in,
        send_sem=half_send,
        recv_sem=half_recv,
        device_id=(sibling, ch),
        device_id_type=MESH,
    )
    half_copy.start()
    half_copy.wait_recv()

    for part in range(2):
        columns = slice(part * half, (part + 1) * half)
        carry = jnp.where(core == part, carry_half[...], carry_in[...])
        decay = jnp.exp(-(rate_ref[:, columns] * float(tokens)))
        entry_states[part] = jnp.where(core == 0, carry, carry * decay + pair_total[part])

    @pl.loop(0, tokens // (2 * BLOCK))
    def _(i):
        start = pl.multiple_of(i * (2 * BLOCK), 2 * BLOCK)
        for part in range(2):
            columns = slice(part * half, (part + 1) * half)
            outs = []
            for sub in range(2):
                entry = entry_states[part]
                entry_states[part] = entry * powers[BLOCK, part]
                state = local_states[2 * i + sub, part] + entry
                rows = driven[pl.ds(pl.multiple_of(start + sub * BLOCK, BLOCK), BLOCK), columns]
                out = taps[0, part] * rows
                for n in range(1, BLOCK):
                    out = out + taps[n, part] * pltpu.roll(rows, n, 0)
                for r in range(order):
                    out = out + response[r, :, columns] * state[r : r + 1, :]
                outs.append(out)
            out = jnp.concatenate(outs, axis=0)
            query = query_buf[pl.ds(start, 2 * BLOCK), columns].astype(jnp.float32)
            gated_ref[pl.ds(start, 2 * BLOCK), columns] = (query * out).astype(gated_ref.dtype)

    for copy in tail_copies + ring_copies + plane_copies + [pair_copy, half_copy]:
        copy.wait_send()


def scan_call(query_input, key_input, value_input, short_kernel, residues, rates):
    nx, ny, nz, nc = SEQ_FACTORS
    tokens, width = query_input.shape
    order = rates.shape[0]
    half = width // 2
    f32 = jnp.float32
    dma = pltpu.SemaphoreType.DMA
    vmem = pl.BlockSpec(memory_space=pltpu.VMEM)
    anywhere = pl.BlockSpec(memory_space=pl.ANY)
    return pl.pallas_call(
        scan_kernel,
        out_shape=jax.ShapeDtypeStruct((tokens, width), jnp.bfloat16),
        in_specs=[anywhere] * 3 + [vmem] * 3,
        out_specs=vmem,
        scratch_shapes=[
            pltpu.VMEM((3, tokens, width), jnp.bfloat16),
            pltpu.VMEM((3, tokens + BLOCK, width), f32),
            pltpu.VMEM((3, TAIL, width), jnp.bfloat16),
            pltpu.VMEM((tokens, width), jnp.bfloat16),
            pltpu.VMEM((tokens, width), f32),
            pltpu.VMEM((tokens // BLOCK, 2, order, half), f32),
            pltpu.VMEM((2, order, half), f32),
            pltpu.VMEM((2, order, half), f32),
            pltpu.VMEM((BLOCK + 1, 2, order, half), f32),
            pltpu.VMEM((order, BLOCK, width), f32),
            pltpu.VMEM((BLOCK, 2, BLOCK, half), f32),
            pltpu.VMEM((2, order, half), f32),
            pltpu.VMEM((2, order, half), f32),
            pltpu.VMEM((nz, order, half), f32),
            pltpu.VMEM((order, half), f32),
            pltpu.VMEM((nx * ny, order, half), f32),
            pltpu.VMEM((order, half), f32),
            pltpu.VMEM((order, half), f32),
            dma((3,)),
            dma((3,)),
            dma((3,)),
            dma,
            dma,
            dma((nz - 1,)),
            dma((nz - 1,)),
            dma((nx * ny - 1,)),
            dma((nx * ny - 1,)),
            dma,
            dma,
        ],
        compiler_params=pltpu.CompilerParams(collective_id=0, has_side_effects=True),
        name="long_scan",
    )(query_input, key_input, value_input, short_kernel, residues, rates)


def per_device(query_input, key_input, value_input, short_kernel, residues, rates, out_weight):
    gated = scan_call(query_input, key_input, value_input, short_kernel, residues, rates)
    return lax.psum_scatter(
        jnp.dot(gated, out_weight, preferred_element_type=jnp.float32).astype(jnp.bfloat16),
        "ch",
        scatter_dimension=0,
        tiled=True,
    ).astype(jnp.float32)


def solution(mesh):
    assert math.prod(SEQ_FACTORS) == mesh.shape["seq"]
    return jax.shard_map(
        per_device,
        mesh=mesh,
        in_specs=(
            P("seq", "ch"),
            P("seq", "ch"),
            P("seq", "ch"),
            P(None, None, "ch"),
            P(None, "ch"),
            P(None, "ch"),
            P("ch", None),
        ),
        out_specs=P(("seq", "ch"), None),
        check_vma=False,
    )
```

profile of v0, /device:TPU:1, one launch (start us, length us, event | category | flops | bytes accessed | tf_op | source)
XLA Modules:
  0.0 87.1 jit_solution(4608213423182479049)
XLA Ops:
  6.5 0.0 reduce-scatter.2.cloned.1.call-start
  6.5 29.0 %long_scan.1 = bf16[128,512]{1,0:T(8,128)(2,1)} custom-call(bf16[128,512]{1,0:T(8,128)(2,1)} %query_hbm.1, bf16[128,512]{1,0:T(8,128)(2,1)} %key_hbm.1, bf16[128,512]{1,0:T(8,128)(2,1)} %value_hbm.1, f32[3,7,512]{2,1,0:T(8,128)} %short_ref.1, f32[16,512]{1,0:T(8,128)} %residue_ref.1, f32[16,512]{1,0:T(8,128)} %rate_ref.1), custom_call_target="tpu_custom_call" | custom-call | tf_op jit(solution)/shard_map/long_scan/pallas_call | solution.py:274
  35.6 6.0 %convolution_convert_fusion = bf16[128,8192]{1,0:T(8,128)(2,1)} fusion(bf16[128,512]{1,0:T(8,128)(2,1)} %long_scan.1, bf16[512,8192]{1,0:T(8,128)(2,1)} %param.13), kind=kOutput, calls=%fused_computation | convolution fusion | flops 1074790400 | bytes 10616832 | tf_op jit(solution)/shard_map/dot_general | solution.py:318
  41.6 0.0 reduce-scatter.2.cloned.1.call-update
  41.6 36.0 %reduce-scatter.2.cloned.1.call-done = bf16[64,8192]{1,0:T(8,128)(2,1)} async-done(((bf16[128,8192]{1,0:T(8,128)(2,1)}), bf16[64,8192]{1,0:T(8,128)(2,1)}) %reduce-scatter.2.cloned.1.call-update) | async-done | bytes 1048592 | tf_op jit(solution)/shard_map/reduce_scatter | solution.py:317
  77.6 2.7 %convert_element_type.7 = f32[64,8192]{1,0:T(8,128)} convert(bf16[64,8192]{1,0:T(8,128)(2,1)} %reduce-scatter.2.cloned.1.call-done) | non-fusion elementwise | flops 524288 | bytes 3145728 | tf_op jit(solution)/shard_map/convert_element_type | solution.py:322
Async XLA Ops:
  6.5 71.1 %reduce-scatter.2.cloned.1.call-start = ((), (), s32[]{:S(2)}) async-start(), calls=%async_computation.1 | async-start | bytes 3145728 | tf_op jit(solution)/shard_map/reduce_scatter | solution.py:317
Sparse Core Ops, SparseCore 0:
  41.7 35.8 reduce-scatter.1
where the time goes:
time: 87.3 us; the launch traced here: 87.1 us
  waiting for transfers between devices  36 us (41%)
  Pallas kernels  29 us (33%)
  between operations  13.4 us (15%)
  matrix products  6.05 us (7%)
  other arithmetic  2.68 us (3%)
    reduce_scatter x1, waiting for transfers between devices, per_device(): lax.psum_scatter(jnp.dot(gated, out_weight, preferred_element_type=jnp.fl...  36 us
    pallas_call x1, Pallas kernels, scan_call(): pl.pallas_call(scan_kernel, out_shape=jax.ShapeDtypeStruct((tokens, width...  29 us
    dot_general x1, matrix products, per_device(): jnp.dot(gated, out_weight, preferred_element_type=jnp.float32)  6.05 us
    convert_element_type x1, other arithmetic, per_device(): return lax.psum_scatter(jnp.dot(gated, out_weight, preferred_element_type...  2.68 us
  transfers between devices with their start and end apart: 1, of which 1 were waited for; matrix products, arithmetic and copies ran while one was open for 0% of the time, Pallas kernels for 0%

commit v1 on v0

--- a/solution.py
+++ b/solution.py
@@ -12,6 +12,17 @@
 MESH = pl.DeviceIdType.MESH
 BLOCK = 8
 TAIL = 16
+COLOURS = 8
+CHUNKS = ((0, 96), (96, 80), (176, 96), (272, 80), (352, 80), (432, 80))
+PARTS = ((0, 176), (176, 176), (352, 160))
+DIRECTIONS = ("x", "y+", "y-", "z+", "z-")
+SECOND = {
+    "x": (-1, 2, "z+"),
+    "y+": (-1, 1, "z+"),
+    "y-": (1, 1, "z-"),
+    "z+": (-2, 0, "y+"),
+    "z-": (2, 0, "y-"),
+}
 
 
 def scan_kernel(
@@ -21,7 +32,14 @@
     short_ref,
     residue_ref,
     rate_ref,
+    weight_hbm,
+    out_ref,
+    own_weight,
+    other_weight,
     gated_ref,
+    rows_in,
+    partial,
+    to_sibling,
     raw,
     ext,
     tails,
@@ -51,6 +69,17 @@
     plane_recv,
     half_send,
     half_recv,
+    weight_sem,
+    cross_send,
+    cross_recv,
+    spread_send,
+    spread_recv,
+    second_send,
+    second_recv,
+    rows_send,
+    rows_recv,
+    result_send,
+    result_recv,
 ):
     nx, ny, nz, nc = SEQ_FACTORS
     planes = nx * ny
@@ -80,10 +109,95 @@
     plane_peers = []
     for step in range(1, planes):
         plane_peers.append((lax.rem(plane + step, planes) * nz + z) * nc + core)
-    peers = [after, before, sibling] + ring_peers + plane_peers
+    x_low = lax.div(plane, ny)
+    y = lax.rem(plane, ny)
+    other = 1 - ch
+
+    def seq_at(x_at, y_at, z_at):
+        return ((x_at * ny + y_at) * nz + z_at) * nc + core
+
+    neighbours = {
+        "x": seq_at(1 - x_low, y, z),
+        "y+": seq_at(x_low, lax.rem(y + 1, ny), z),
+        "y-": seq_at(x_low, lax.rem(y + ny - 1, ny), z),
+        "z+": seq_at(x_low, y, lax.rem(z + 1, nz)),
+        "z-": seq_at(x_low, y, lax.rem(z + nz - 1, nz)),
+    }
+    across = neighbours["x"]
+    peers = [(peer, ch) for peer in [after, before, sibling] + ring_peers + plane_peers]
+    peers += [(across, other), (me, other), (sibling, other)]
     barrier = pltpu.get_barrier_semaphore()
     for peer in peers:
-        pl.semaphore_signal(barrier, inc=1, device_id=(peer, ch), device_id_type=MESH)
+        pl.semaphore_signal(barrier, inc=1, device_id=peer, device_id_type=MESH)
+
+    depth, own_columns = own_weight.shape
+    piece_columns = own_columns // COLOURS
+    first_column = core * own_columns
+    colour = lax.rem(4 * x_low + 2 * y + z, COLOURS)
+
+    def shifted(by):
+        return lax.rem(colour + by + COLOURS, COLOURS)
+
+    weight_copy = pltpu.make_async_copy(
+        weight_hbm.at[:, pl.ds(pl.multiple_of(first_column, own_columns), own_columns)],
+        own_weight,
+        weight_sem,
+    )
+
+    def cross_copy(at, piece, start, size):
+        column = pl.multiple_of(first_column + piece * piece_columns, piece_columns)
+        return pltpu.make_async_remote_copy(
+            src_ref=weight_hbm.at[pl.ds(start, size), pl.ds(column, piece_columns)],
+            dst_ref=other_weight.at[piece, pl.ds(start, size)],
+            send_sem=cross_send.at[at],
+            recv_sem=cross_recv.at[at],
+            device_id=(across, other),
+            device_id_type=MESH,
+        )
+
+    cross_copies = [
+        cross_copy(at, shifted(4), start, size) for at, (start, size) in enumerate(CHUNKS)
+    ]
+    cross_copies.append(cross_copy(len(CHUNKS), shifted(1), *PARTS[2]))
+
+    def passed_on(direction, piece, start, size, send_sem, recv_sem):
+        return pltpu.make_async_remote_copy(
+            src_ref=other_weight.at[piece, pl.ds(start, size)],
+            dst_ref=other_weight.at[piece, pl.ds(start, size)],
+            send_sem=send_sem,
+            recv_sem=recv_sem,
+            device_id=(neighbours[direction], ch),
+            device_id_type=MESH,
+        )
+
+    spread_copies = {}
+    second_copies = {}
+    for to, direction in enumerate(DIRECTIONS):
+        for at, (start, size) in enumerate(CHUNKS):
+            spread_copies[direction, at] = passed_on(
+                direction, colour, start, size, spread_send.at[to, at], spread_recv.at[to, at]
+            )
+        by, part, _ = SECOND[direction]
+        second_copies[direction] = passed_on(
+            direction, shifted(by), *PARTS[part], second_send.at[to], second_recv.at[to]
+        )
+
+    def spread(at):
+        cross_copies[at].wait_recv()
+        for direction in DIRECTIONS:
+            spread_copies[direction, at].start()
+
+    def second_hop(part):
+        for direction in DIRECTIONS:
+            by, its_part, came = SECOND[direction]
+            if its_part == part:
+                for at in (2 * part, 2 * part + 1):
+                    if (came, at) not in arrived:
+                        arrived.add((came, at))
+                        spread_copies[came, at].wait_recv()
+                second_copies[direction].start()
+
+    arrived = set()
 
     for part in range(2):
         columns = slice(part * half, (part + 1) * half)
@@ -119,6 +233,9 @@
         )
         copy.start()
         tail_copies.append(copy)
+    for copy in cross_copies:
+        copy.start()
+    weight_copy.start()
     for copy in tail_copies:
         copy.wait_recv()
     for at in range(3):
@@ -166,6 +283,7 @@
         start = pl.multiple_of(i * (2 * BLOCK), 2 * BLOCK)
         query_buf[pl.ds(start, 2 * BLOCK)] = short_rows(2, 0, start).astype(query_buf.dtype)
 
+    spread(0)
     pair_copy.wait_recv()
     my_rates = jnp.where(core == 0, rate_ref[:, 0:half], rate_ref[:, half:])
     mine = own_total[core]
@@ -187,6 +305,8 @@
         )
         copy.start()
         ring_copies.append(copy)
+    spread(1)
+    spread(2)
     for copy in ring_copies:
         copy.wait_recv()
     chip_decay = jnp.exp(-(my_rates * float(tokens * nc)))
@@ -209,6 +329,8 @@
         )
         copy.start()
         plane_copies.append(copy)
+    spread(3)
+    spread(4)
     for copy in plane_copies:
         copy.wait_recv()
     row_decay = jnp.exp(-(my_rates * float(tokens * nc * nz)))
@@ -229,6 +351,8 @@
         device_id_type=MESH,
     )
     half_copy.start()
+    spread(5)
+    second_hop(0)
     half_copy.wait_recv()
 
     for part in range(2):
@@ -258,25 +382,105 @@
             query = query_buf[pl.ds(start, 2 * BLOCK), columns].astype(jnp.float32)
             gated_ref[pl.ds(start, 2 * BLOCK), columns] = (query * out).astype(gated_ref.dtype)
 
+    out_rows = tokens // 2
+    keep = pl.multiple_of(ch * out_rows, out_rows)
+    give = pl.multiple_of(other * out_rows, out_rows)
+    rows_copies = []
+    for at, (source, slot, place, target) in enumerate(
+        (
+            (give, 1, 0, (me, other)),
+            (give, 1, 1, (sibling, other)),
+            (keep, 0, 1, (sibling, ch)),
+        )
+    ):
+        copy = pltpu.make_async_remote_copy(
+            src_ref=gated_ref.at[pl.ds(source, out_rows)],
+            dst_ref=rows_in.at[slot, pl.ds(place * out_rows, out_rows)],
+            send_sem=rows_send.at[at],
+            recv_sem=rows_recv.at[at],
+            device_id=target,
+            device_id_type=MESH,
+        )
+        copy.start()
+        rows_copies.append(copy)
+    second_hop(1)
+    second_hop(2)
+    rows_in[0, 0:out_rows] = gated_ref[pl.ds(keep, out_rows)]
+    weight_copy.wait()
+    rows_copies[2].wait_recv()
+
+    @pl.loop(0, COLOURS)
+    def _(n):
+        columns = pl.ds(pl.multiple_of(n * piece_columns, piece_columns), piece_columns)
+        partial[n] = jnp.dot(rows_in[0], own_weight[:, columns], preferred_element_type=jnp.float32)
+
+    for direction in DIRECTIONS:
+        for at in range(len(CHUNKS)):
+            if (direction, at) not in arrived:
+                spread_copies[direction, at].wait_recv()
+        second_copies[direction].wait_recv()
+    cross_copies[-1].wait_recv()
+    rows_copies[0].wait_recv()
+    rows_copies[1].wait_recv()
+
+    def result_copy(n):
+        column = pl.multiple_of(first_column + n * piece_columns, piece_columns)
+        return pltpu.make_async_remote_copy(
+            src_ref=to_sibling.at[n],
+            dst_ref=out_ref.at[:, pl.ds(column, piece_columns)],
+            send_sem=result_send.at[n],
+            recv_sem=result_recv.at[n],
+            device_id=(sibling, ch),
+            device_id_type=MESH,
+        )
+
+    @pl.loop(0, COLOURS)
+    def _(n):
+        column = pl.multiple_of(first_column + n * piece_columns, piece_columns)
+        total = partial[n] + jnp.dot(
+            rows_in[1], other_weight[n], preferred_element_type=jnp.float32
+        )
+        to_sibling[n] = total[out_rows:]
+        result_copy(n).start()
+        out_ref[:, pl.ds(column, piece_columns)] = total[:out_rows]
+
+    @pl.loop(0, COLOURS)
+    def _(n):
+        result_copy(n).wait()
+
     for copy in tail_copies + ring_copies + plane_copies + [pair_copy, half_copy]:
         copy.wait_send()
-
-
-def scan_call(query_input, key_input, value_input, short_kernel, residues, rates):
+    for copy in cross_copies + rows_copies:
+        copy.wait_send()
+    for copy in list(spread_copies.values()) + list(second_copies.values()):
+        copy.wait_send()
+
+
+def scan_call(query_input, key_input, value_input, short_kernel, residues, rates, out_weight):
     nx, ny, nz, nc = SEQ_FACTORS
     tokens, width = query_input.shape
     order = rates.shape[0]
     half = width // 2
+    columns = out_weight.shape[1]
+    out_rows = tokens // 2
+    piece_columns = columns // nc // COLOURS
     f32 = jnp.float32
+    bf16 = jnp.bfloat16
     dma = pltpu.SemaphoreType.DMA
     vmem = pl.BlockSpec(memory_space=pltpu.VMEM)
     anywhere = pl.BlockSpec(memory_space=pl.ANY)
     return pl.pallas_call(
         scan_kernel,
-        out_shape=jax.ShapeDtypeStruct((tokens, width), jnp.bfloat16),
-        in_specs=[anywhere] * 3 + [vmem] * 3,
+        out_shape=jax.ShapeDtypeStruct((out_rows, columns), f32),
+        in_specs=[anywhere] * 3 + [vmem] * 3 + [anywhere],
         out_specs=vmem,
         scratch_shapes=[
+            pltpu.VMEM((width, columns // nc), bf16),
+            pltpu.VMEM((COLOURS, width, piece_columns), bf16),
+            pltpu.VMEM((tokens, width), bf16),
+            pltpu.VMEM((2, tokens, width), bf16),
+            pltpu.VMEM((COLOURS, tokens, piece_columns), f32),
+            pltpu.VMEM((COLOURS, out_rows, piece_columns), f32),
             pltpu.VMEM((3, tokens, width), jnp.bfloat16),
             pltpu.VMEM((3, tokens + BLOCK, width), f32),
             pltpu.VMEM((3, TAIL, width), jnp.bfloat16),
@@ -306,20 +510,27 @@
             dma((nx * ny - 1,)),
             dma,
             dma,
+            dma,
+            dma((len(CHUNKS) + 1,)),
+            dma((len(CHUNKS) + 1,)),
+            dma((len(DIRECTIONS), len(CHUNKS))),
+            dma((len(DIRECTIONS), len(CHUNKS))),
+            dma((len(DIRECTIONS),)),
+            dma((len(DIRECTIONS),)),
+            dma((3,)),
+            dma((3,)),
+            dma((COLOURS,)),
+            dma((COLOURS,)),
         ],
         compiler_params=pltpu.CompilerParams(collective_id=0, has_side_effects=True),
         name="long_scan",
-    )(query_input, key_input, value_input, short_kernel, residues, rates)
+    )(query_input, key_input, value_input, short_kernel, residues, rates, out_weight)
 
 
 def per_device(query_input, key_input, value_input, short_kernel, residues, rates, out_weight):
-    gated = scan_call(query_input, key_input, value_input, short_kernel, residues, rates)
-    return lax.psum_scatter(
-        jnp.dot(gated, out_weight, preferred_element_type=jnp.float32).astype(jnp.bfloat16),
-        "ch",
-        scatter_dimension=0,
-        tiled=True,
-    ).astype(jnp.float32)
+    return scan_call(
+        query_input, key_input, value_input, short_kernel, residues, rates, out_weight
+    )
 
 
 def solution(mesh):

time: 87.3 us -> 47.9 us (0.55)
  waiting for transfers between devices: 36 us -> 0 us
  Pallas kernels: 29 us -> 44.7 us
  between operations: 13.4 us -> 0.01 us
  matrix products: 6.05 us -> 0 us
  local copies, waits for them, and re-layouts: 0 us -> 3.06 us
  other arithmetic: 2.68 us -> 0 us
    reduce_scatter x1 -> x0, waiting for transfers between devices: 36 us -> none  [per_device(): lax.psum_scatter(jnp.dot(gated, out_weight, preferred_element_type=jnp.fl...]
    pallas_call x1, Pallas kernels: 29 us -> 44.7 us  [scan_call(): pl.pallas_call(scan_kernel, out_shape=jax.ShapeDtypeStruct((out_rows, col...]
    dot_general x1 -> x0, matrix products: 6.05 us -> none  [per_device(): jnp.dot(gated, out_weight, preferred_element_type=jnp.float32)]
    unnamed x0 -> x1, local copies, waits for them, and re-layouts: none -> 3.06 us
    convert_element_type x1 -> x0, other arithmetic: 2.68 us -> none  [per_device(): return lax.psum_scatter(jnp.dot(gated, out_weight, preferred_element_type...]
  transfers between devices with their start and end apart: 1 -> 0, of which waited for: 1 -> 0; matrix products, arithmetic and copies ran while one was open for 0% -> 0% of each run, Pallas kernels for 0% -> 0%
where the time goes in v1:
time: 47.9 us; the launch traced here: 47.8 us
  Pallas kernels  44.7 us (93%)
  local copies, waits for them, and re-layouts  3.06 us (6%)
    pallas_call x1, Pallas kernels, scan_call(): pl.pallas_call(scan_kernel, out_shape=jax.ShapeDtypeStruct((out_rows, col...  44.7 us
    unnamed x1, local copies, waits for them, and re-layouts  3.06 us

profile of v1, /device:TPU:1, one launch (start us, length us, event | category | flops | bytes accessed | tf_op | source)
XLA Modules:
  0.0 47.8 jit_solution(10519153093178224488)
XLA Ops:
  0.0 44.7 %long_scan.1 = f32[64,8192]{1,0:T(8,128)} custom-call(bf16[128,512]{1,0:T(8,128)(2,1)} %query_hbm.1, bf16[128,512]{1,0:T(8,128)(2,1)} %key_hbm.1, bf16[128,512]{1,0:T(8,128)(2,1)} %value_hbm.1, f32[3,7,512]{2,1,0:T(8,128)} %short_ref.1, f32[16,512]{1,0:T(8,128)} %residue_ref.1, f32[16,512]{1,0:T(8,128)} %rate_ref.1, bf16[512,8192]{1,0:T(8,128)(2,1)} %weight_hbm.1), custom_call_target="tpu_custom_call" | custom-call | tf_op jit(solution)/shard_map/long_scan/pallas_call | solution.py:472
  44.7 3.1 %copy.9 = f32[64,8192]{1,0:T(8,128)} copy(f32[64,8192]{1,0:T(8,128)} %long_scan.1) | data formatting | bytes 4194304

commit v2 on v1

--- a/solution.py
+++ b/solution.py
@@ -125,7 +125,7 @@
     }
     across = neighbours["x"]
     peers = [(peer, ch) for peer in [after, before, sibling] + ring_peers + plane_peers]
-    peers += [(across, other), (me, other), (sibling, other)]
+    peers += [(across, other), (me, other)]
     barrier = pltpu.get_barrier_semaphore()
     for peer in peers:
         pl.semaphore_signal(barrier, inc=1, device_id=peer, device_id_type=MESH)
@@ -184,6 +184,8 @@
 
     def spread(at):
         cross_copies[at].wait_recv()
+        if at + 2 < len(cross_copies):
+            cross_copies[at + 2].start()
         for direction in DIRECTIONS:
             spread_copies[direction, at].start()
 
@@ -203,20 +205,24 @@
         columns = slice(part * half, (part + 1) * half)
         decay = jnp.exp(-rate_ref[:, columns])
         power = jnp.ones_like(decay)
-        scaled = residue_ref[:, columns] * jnp.sqrt(2.0 * rate_ref[:, columns])
-        for n in range(BLOCK):
+        for n in range(BLOCK + 1):
             powers[n, part] = power
-            tap = jnp.sum(scaled * power, axis=0, keepdims=True)
+            power = power * decay
+    order = rate_ref.shape[0]
+
+    def output_tables():
+        for part in range(2):
+            columns = slice(part * half, (part + 1) * half)
+            scaled = residue_ref[:, columns] * jnp.sqrt(2.0 * rate_ref[:, columns])
             rows = lax.broadcasted_iota(jnp.int32, (BLOCK, half), 0)
-            taps[n, part] = jnp.where(rows >= n, jnp.broadcast_to(tap, (BLOCK, half)), 0.0)
-            power = power * decay
-        powers[BLOCK, part] = power
-    ages = lax.broadcasted_iota(jnp.int32, (BLOCK, width), 0).astype(jnp.float32) + 1.0
-    order = rate_ref.shape[0]
-    for r in range(order):
-        rate_row = rate_ref[r : r + 1, :]
-        scale_row = residue_ref[r : r + 1, :] * jnp.sqrt(2.0 * rate_row)
-        response[r] = scale_row * jnp.exp(-(ages * rate_row))
+            for n in range(BLOCK):
+                tap = jnp.sum(scaled * powers[n, part], axis=0, keepdims=True)
+                taps[n, part] = jnp.where(rows >= n, jnp.broadcast_to(tap, (BLOCK, half)), 0.0)
+        ages = lax.broadcasted_iota(jnp.int32, (BLOCK, width), 0).astype(jnp.float32) + 1.0
+        for r in range(order):
+            rate_row = rate_ref[r : r + 1, :]
+            scale_row = residue_ref[r : r + 1, :] * jnp.sqrt(2.0 * rate_row)
+            response[r] = scale_row * jnp.exp(-(ages * rate_row))
 
     pl.semaphore_wait(barrier, len(peers))
     for copy in loads:
@@ -233,7 +239,7 @@
         )
         copy.start()
         tail_copies.append(copy)
-    for copy in cross_copies:
+    for copy in cross_copies[:2]:
         copy.start()
     weight_copy.start()
     for copy in tail_copies:
@@ -305,6 +311,7 @@
         )
         copy.start()
         ring_copies.append(copy)
+    output_tables()
     spread(1)
     spread(2)
     for copy in ring_copies:
@@ -331,6 +338,8 @@
         plane_copies.append(copy)
     spread(3)
     spread(4)
+    second_hop(0)
+    spread(5)
     for copy in plane_copies:
         copy.wait_recv()
     row_decay = jnp.exp(-(my_rates * float(tokens * nc * nz)))
@@ -351,77 +360,90 @@
         device_id_type=MESH,
     )
     half_copy.start()
-    spread(5)
-    second_hop(0)
+    second_hop(1)
     half_copy.wait_recv()
 
+    entries = []
     for part in range(2):
         columns = slice(part * half, (part + 1) * half)
         carry = jnp.where(core == part, carry_half[...], carry_in[...])
         decay = jnp.exp(-(rate_ref[:, columns] * float(tokens)))
-        entry_states[part] = jnp.where(core == 0, carry, carry * decay + pair_total[part])
-
-    @pl.loop(0, tokens // (2 * BLOCK))
-    def _(i):
-        start = pl.multiple_of(i * (2 * BLOCK), 2 * BLOCK)
+        entries.append(jnp.where(core == 0, carry, carry * decay + pair_total[part]))
+    out_rows = tokens // 2
+    steps = out_rows // (2 * BLOCK)
+
+    def output_half(which):
         for part in range(2):
             columns = slice(part * half, (part + 1) * half)
-            outs = []
-            for sub in range(2):
-                entry = entry_states[part]
-                entry_states[part] = entry * powers[BLOCK, part]
-                state = local_states[2 * i + sub, part] + entry
-                rows = driven[pl.ds(pl.multiple_of(start + sub * BLOCK, BLOCK), BLOCK), columns]
-                out = taps[0, part] * rows
-                for n in range(1, BLOCK):
-                    out = out + taps[n, part] * pltpu.roll(rows, n, 0)
-                for r in range(order):
-                    out = out + response[r, :, columns] * state[r : r + 1, :]
-                outs.append(out)
-            out = jnp.concatenate(outs, axis=0)
-            query = query_buf[pl.ds(start, 2 * BLOCK), columns].astype(jnp.float32)
-            gated_ref[pl.ds(start, 2 * BLOCK), columns] = (query * out).astype(gated_ref.dtype)
-
-    out_rows = tokens // 2
+            decay = jnp.exp(-(rate_ref[:, columns] * float(out_rows)))
+            entry_states[part] = jnp.where(which == 0, entries[part], entries[part] * decay)
+
+        @pl.loop(0, steps)
+        def _(step):
+            i = which * steps + step
+            start = pl.multiple_of(i * (2 * BLOCK), 2 * BLOCK)
+            for part in range(2):
+                columns = slice(part * half, (part + 1) * half)
+                outs = []
+                for sub in range(2):
+                    entry = entry_states[part]
+                    entry_states[part] = entry * powers[BLOCK, part]
+                    state = local_states[2 * i + sub, part] + entry
+                    rows = driven[pl.ds(pl.multiple_of(start + sub * BLOCK, BLOCK), BLOCK), columns]
+                    out = taps[0, part] * rows
+                    for n in range(1, BLOCK):
+                        out = out + taps[n, part] * pltpu.roll(rows, n, 0)
+                    for r in range(order):
+                        out = out + response[r, :, columns] * state[r : r + 1, :]
+                    outs.append(out)
+                out = jnp.concatenate(outs, axis=0)
+                query = query_buf[pl.ds(start, 2 * BLOCK), columns].astype(jnp.float32)
+                gated_ref[pl.ds(start, 2 * BLOCK), columns] = (query * out).astype(gated_ref.dtype)
+
     keep = pl.multiple_of(ch * out_rows, out_rows)
     give = pl.multiple_of(other * out_rows, out_rows)
+    arriving = rows_in.at[1, pl.ds(0, out_rows)]
     rows_copies = []
     for at, (source, slot, place, target) in enumerate(
         (
-            (give, 1, 0, (me, other)),
-            (give, 1, 1, (sibling, other)),
-            (keep, 0, 1, (sibling, ch)),
+            (gated_ref.at[pl.ds(give, out_rows)], 1, 0, (me, other)),
+            (gated_ref.at[pl.ds(keep, out_rows)], 0, 1, (sibling, ch)),
+            (arriving, 1, 1, (sibling, ch)),
         )
     ):
-        copy = pltpu.make_async_remote_copy(
-            src_ref=gated_ref.at[pl.ds(source, out_rows)],
-            dst_ref=rows_in.at[slot, pl.ds(place * out_rows, out_rows)],
-            send_sem=rows_send.at[at],
-            recv_sem=rows_recv.at[at],
-            device_id=target,
-            device_id_type=MESH,
-        )
-        copy.start()
-        rows_copies.append(copy)
-    second_hop(1)
+        rows_copies.append(
+            pltpu.make_async_remote_copy(
+                src_ref=source,
+                dst_ref=rows_in.at[slot, pl.ds(place * out_rows, out_rows)],
+                send_sem=rows_send.at[at],
+                recv_sem=rows_recv.at[at],
+                device_id=target,
+                device_id_type=MESH,
+            )
+        )
+    output_half(other)
+    rows_copies[0].start()
     second_hop(2)
+    output_half(ch)
+    rows_copies[1].start()
     rows_in[0, 0:out_rows] = gated_ref[pl.ds(keep, out_rows)]
     weight_copy.wait()
-    rows_copies[2].wait_recv()
+    rows_copies[1].wait_recv()
 
     @pl.loop(0, COLOURS)
     def _(n):
         columns = pl.ds(pl.multiple_of(n * piece_columns, piece_columns), piece_columns)
         partial[n] = jnp.dot(rows_in[0], own_weight[:, columns], preferred_element_type=jnp.float32)
 
+    rows_copies[0].wait_recv()
+    rows_copies[2].start()
     for direction in DIRECTIONS:
         for at in range(len(CHUNKS)):
             if (direction, at) not in arrived:
                 spread_copies[direction, at].wait_recv()
         second_copies[direction].wait_recv()
     cross_copies[-1].wait_recv()
-    rows_copies[0].wait_recv()
-    rows_copies[1].wait_recv()
+    rows_copies[2].wait_recv()
 
     def result_copy(n):
         column = pl.multiple_of(first_column + n * piece_columns, piece_columns)
@@ -440,6 +462,7 @@
         total = partial[n] + jnp.dot(
             rows_in[1], other_weight[n], preferred_element_type=jnp.float32
         )
+        total = total.astype(out_ref.dtype)
         to_sibling[n] = total[out_rows:]
         result_copy(n).start()
         out_ref[:, pl.ds(column, piece_columns)] = total[:out_rows]
@@ -471,7 +494,7 @@
     anywhere = pl.BlockSpec(memory_space=pl.ANY)
     return pl.pallas_call(
         scan_kernel,
-        out_shape=jax.ShapeDtypeStruct((out_rows, columns), f32),
+        out_shape=jax.ShapeDtypeStruct((out_rows, columns), bf16),
         in_specs=[anywhere] * 3 + [vmem] * 3 + [anywhere],
         out_specs=vmem,
         scratch_shapes=[
@@ -480,7 +503,7 @@
             pltpu.VMEM((tokens, width), bf16),
             pltpu.VMEM((2, tokens, width), bf16),
             pltpu.VMEM((COLOURS, tokens, piece_columns), f32),
-            pltpu.VMEM((COLOURS, out_rows, piece_columns), f32),
+            pltpu.VMEM((COLOURS, out_rows, piece_columns), bf16),
             pltpu.VMEM((3, tokens, width), jnp.bfloat16),
             pltpu.VMEM((3, tokens + BLOCK, width), f32),
             pltpu.VMEM((3, TAIL, width), jnp.bfloat16),
@@ -528,9 +551,10 @@
 
 
 def per_device(query_input, key_input, value_input, short_kernel, residues, rates, out_weight):
-    return scan_call(
+    mixed = scan_call(
         query_input, key_input, value_input, short_kernel, residues, rates, out_weight
     )
+    return mixed.astype(jnp.float32)
 
 
 def solution(mesh):

time: 47.9 us -> 47 us (0.981)
  local copies, waits for them, and re-layouts: 3.06 us -> 0 us
  other arithmetic: 0 us -> 2.68 us
  Pallas kernels: 44.7 us -> 44.1 us
    unnamed x1 -> x0, local copies, waits for them, and re-layouts: 3.06 us -> none
    convert_element_type x0 -> x1, other arithmetic: none -> 2.68 us  [per_device(): return mixed.astype(jnp.float32)]
    pallas_call x1, Pallas kernels: 44.7 us -> 44.1 us  [scan_call(): pl.pallas_call(scan_kernel, out_shape=jax.ShapeDtypeStruct((out_rows, col...]
where the time goes in v2:
time: 47 us; the launch traced here: 46.8 us
  Pallas kernels  44.1 us (94%)
  other arithmetic  2.68 us (6%)
    pallas_call x1, Pallas kernels, scan_call(): pl.pallas_call(scan_kernel, out_shape=jax.ShapeDtypeStruct((out_rows, col...  44.1 us
    convert_element_type x1, other arithmetic, per_device(): return mixed.astype(jnp.float32)  2.68 us

profile of v2, /device:TPU:1, one launch (start us, length us, event | category | flops | bytes accessed | tf_op | source)
XLA Modules:
  0.0 46.8 jit_solution(17085860044464216849)
XLA Ops:
  0.0 44.1 %long_scan.1 = bf16[64,8192]{1,0:T(8,128)(2,1)} custom-call(bf16[128,512]{1,0:T(8,128)(2,1)} %query_hbm.1, bf16[128,512]{1,0:T(8,128)(2,1)} %key_hbm.1, bf16[128,512]{1,0:T(8,128)(2,1)} %value_hbm.1, f32[3,7,512]{2,1,0:T(8,128)} %short_ref.1, f32[16,512]{1,0:T(8,128)} %residue_ref.1, f32[16,512]{1,0:T(8,128)} %rate_ref.1, bf16[512,8192]{1,0:T(8,128)(2,1)} %weight_hbm.1), custom_call_target="tpu_custom_call" | custom-call | tf_op jit(solution)/shard_map/long_scan/pallas_call | solution.py:495
  44.1 2.7 %convert_element_type.3 = f32[64,8192]{1,0:T(8,128)} convert(bf16[64,8192]{1,0:T(8,128)(2,1)} %long_scan.1) | non-fusion elementwise | flops 524288 | bytes 3145728 | tf_op jit(solution)/shard_map/convert_element_type | solution.py:557

commit v3 on v2

--- a/solution.py
+++ b/solution.py
@@ -108,7 +108,7 @@
         ring_peers.append((plane * nz + lax.rem(z + step, nz)) * nc + core)
     plane_peers = []
     for step in range(1, planes):
-        plane_peers.append((lax.rem(plane + step, planes) * nz + z) * nc + core)
+        plane_peers.append((lax.rem(plane + step, planes) * nz + z) * nc)
     x_low = lax.div(plane, ny)
     y = lax.rem(plane, ny)
     other = 1 - ch
@@ -124,7 +124,8 @@
         "z-": seq_at(x_low, y, lax.rem(z + nz - 1, nz)),
     }
     across = neighbours["x"]
-    peers = [(peer, ch) for peer in [after, before, sibling] + ring_peers + plane_peers]
+    peers = [(peer, ch) for peer in [after, before, sibling] + ring_peers]
+    peers += [(peer + at, ch) for peer in plane_peers for at in range(nc)]
     peers += [(across, other), (me, other)]
     barrier = pltpu.get_barrier_semaphore()
     for peer in peers:
@@ -322,34 +323,8 @@
     for at in range(nz):
         before_me = jnp.where(at == z, total, before_me)
         total = total * chip_decay + ring_in[at]
-    plane_in[plane] = total
-
-    plane_copies = []
-    for at, peer in enumerate(plane_peers):
-        copy = pltpu.make_async_remote_copy(
-            src_ref=plane_in.at[plane],
-            dst_ref=plane_in.at[plane],
-            send_sem=plane_send.at[at],
-            recv_sem=plane_recv.at[at],
-            device_id=(peer, ch),
-            device_id_type=MESH,
-        )
-        copy.start()
-        plane_copies.append(copy)
-    spread(3)
-    spread(4)
-    second_hop(0)
-    spread(5)
-    for copy in plane_copies:
-        copy.wait_recv()
-    row_decay = jnp.exp(-(my_rates * float(tokens * nc * nz)))
-    total = jnp.zeros((order, half), jnp.float32)
-    earlier = total
-    for at in range(planes):
-        earlier = jnp.where(at == plane, total, earlier)
-        total = total * row_decay + plane_in[at]
-    distance = (z * (tokens * nc)).astype(jnp.float32)
-    carry_half[...] = before_me + earlier * jnp.exp(-(my_rates * distance))
+    plane_in[core, plane] = total
+    carry_half[...] = before_me
 
     half_copy = pltpu.make_async_remote_copy(
         src_ref=carry_half,
@@ -360,13 +335,47 @@
         device_id_type=MESH,
     )
     half_copy.start()
+
+    def plane_copy(step, to_core, part):
+        return pltpu.make_async_remote_copy(
+            src_ref=plane_in.at[part, plane],
+            dst_ref=plane_in.at[part, plane],
+            send_sem=plane_send.at[step - 1, to_core],
+            recv_sem=plane_recv.at[step - 1, part],
+            device_id=(plane_peers[step - 1] + to_core, ch),
+            device_id_type=MESH,
+        )
+
+    for step in range(1, planes):
+
+        @pl.when(plane + step < planes)
+        def _():
+            for to_core in range(nc):
+                plane_copy(step, to_core, core).start()
+
+    spread(3)
+    spread(4)
+    second_hop(0)
+    spread(5)
     second_hop(1)
     half_copy.wait_recv()
-
+    for step in range(1, planes):
+
+        @pl.when(plane >= step)
+        def _():
+            for part in range(nc):
+                plane_copy(step, 0, part).wait_recv()
+
+    distance = (z * (tokens * nc)).astype(jnp.float32)
     entries = []
     for part in range(2):
         columns = slice(part * half, (part + 1) * half)
+        row_decay = jnp.exp(-(rate_ref[:, columns] * float(tokens * nc * nz)))
+        earlier = jnp.zeros((order, half), jnp.float32)
+        for at in range(planes - 1):
+            earlier = jnp.where(at < plane, earlier * row_decay + plane_in[part, at], earlier)
         carry = jnp.where(core == part, carry_half[...], carry_in[...])
+        carry = carry + earlier * jnp.exp(-(rate_ref[:, columns] * distance))
         decay = jnp.exp(-(rate_ref[:, columns] * float(tokens)))
         entries.append(jnp.where(core == 0, carry, carry * decay + pair_total[part]))
     out_rows = tokens // 2
@@ -471,7 +480,14 @@
     def _(n):
         result_copy(n).wait()
 
-    for copy in tail_copies + ring_copies + plane_copies + [pair_copy, half_copy]:
+    for step in range(1, planes):
+
+        @pl.when(plane + step < planes)
+        def _():
+            for to_core in range(nc):
+                plane_copy(step, to_core, core).wait_send()
+
+    for copy in tail_copies + ring_copies + [pair_copy, half_copy]:
         copy.wait_send()
     for copy in cross_copies + rows_copies:
         copy.wait_send()
@@ -519,7 +535,7 @@
             pltpu.VMEM((2, order, half), f32),
             pltpu.VMEM((nz, order, half), f32),
             pltpu.VMEM((order, half), f32),
-            pltpu.VMEM((nx * ny, order, half), f32),
+            pltpu.VMEM((nc, nx * ny, order, half), f32),
             pltpu.VMEM((order, half), f32),
             pltpu.VMEM((order, half), f32),
             dma((3,)),
@@ -529,8 +545,8 @@
             dma,
             dma((nz - 1,)),
             dma((nz - 1,)),
-            dma((nx * ny - 1,)),
-            dma((nx * ny - 1,)),
+            dma((nx * ny - 1, nc)),
+            dma((nx * ny - 1, nc)),
             dma,
             dma,
             dma,
@@ -545,7 +561,7 @@
             dma((COLOURS,)),
             dma((COLOURS,)),
         ],
-        compiler_params=pltpu.CompilerParams(collective_id=0, has_side_effects=True),
+        compiler_params=pltpu.CompilerParams(collective_id=0, has_side_effects=True, vmem_limit_bytes=48 << 20),
         name="long_scan",
     )(query_input, key_input, value_input, short_kernel, residues, rates, out_weight)
 

time: 47 us -> 51.3 us (1.091)
  local copies, waits for them, and re-layouts: 0 us -> 5.02 us
  other arithmetic: 2.68 us -> 1.46 us
    unnamed x0 -> x12, local copies, waits for them, and re-layouts: none -> 5.02 us
    convert_element_type x1, other arithmetic: 2.68 us -> 1.46 us  [per_device(): return mixed.astype(jnp.float32)]
where the time goes in v3:
time: 51.3 us; the launch traced here: 50.9 us
  Pallas kernels  44.4 us (87%)
  local copies, waits for them, and re-layouts  5.02 us (10%)
  other arithmetic  1.46 us (3%)
    pallas_call x1, Pallas kernels, scan_call(): pl.pallas_call(scan_kernel, out_shape=jax.ShapeDtypeStruct((out_rows, col...  44.4 us
    unnamed x12, local copies, waits for them, and re-layouts  5.02 us
    convert_element_type x1, other arithmetic, per_device(): return mixed.astype(jnp.float32)  1.46 us

profile of v3, /device:TPU:1, one launch (start us, length us, event | category | flops | bytes accessed | tf_op | source)
XLA Modules:
  0.0 50.9 jit_solution(6947441927324591579)
XLA Ops:
  0.0 0.0 copy-start
  0.0 0.9 %copy-done = bf16[128,512]{1,0:T(8,128)(2,1)S(1)} copy-done((bf16[128,512]{1,0:T(8,128)(2,1)S(1)}, bf16[128,512]{1,0:T(8,128)(2,1)}, u32[]{:S(2)}) %copy-start) | copy-done | bytes 131096
  0.9 0.0 copy-start.1
  0.9 0.9 %copy-done.1 = bf16[128,512]{1,0:T(8,128)(2,1)S(1)} copy-done((bf16[128,512]{1,0:T(8,128)(2,1)S(1)}, bf16[128,512]{1,0:T(8,128)(2,1)}, u32[]{:S(2)}) %copy-start.1) | copy-done | bytes 131096
  1.8 0.0 copy-start.2
  1.8 0.9 %copy-done.2 = bf16[128,512]{1,0:T(8,128)(2,1)S(1)} copy-done((bf16[128,512]{1,0:T(8,128)(2,1)S(1)}, bf16[128,512]{1,0:T(8,128)(2,1)}, u32[]{:S(2)}) %copy-start.2) | copy-done | bytes 131096
  2.7 0.0 copy-start.3
  2.7 0.8 %copy-done.3 = f32[3,7,512]{2,1,0:T(8,128)S(1)} copy-done((f32[3,7,512]{2,1,0:T(8,128)S(1)}, f32[3,7,512]{2,1,0:T(8,128)}, u32[]{:S(2)}) %copy-start.3) | copy-done | bytes 43032
  3.5 0.0 copy-start.4
  3.5 0.8 %copy-done.4 = f32[16,512]{1,0:T(8,128)S(1)} copy-done((f32[16,512]{1,0:T(8,128)S(1)}, f32[16,512]{1,0:T(8,128)}, u32[]{:S(2)}) %copy-start.4) | copy-done | bytes 32792
  4.3 0.0 copy-start.5
  4.3 0.8 %copy-done.5 = f32[16,512]{1,0:T(8,128)S(1)} copy-done((f32[16,512]{1,0:T(8,128)S(1)}, f32[16,512]{1,0:T(8,128)}, u32[]{:S(2)}) %copy-start.5) | copy-done | bytes 32792
  5.0 44.4 %long_scan.1 = bf16[64,8192]{1,0:T(8,128)(2,1)S(1)} custom-call(bf16[128,512]{1,0:T(8,128)(2,1)S(1)} %copy-done, bf16[128,512]{1,0:T(8,128)(2,1)S(1)} %copy-done.1, bf16[128,512]{1,0:T(8,128)(2,1)S(1)} %copy-done.2, f32[3,7,512]{2,1,0:T(8,128)S(1)} %copy-done.3, f32[16,512]{1,0:T(8,128)S(1)} %copy-done.4, f32[16,512]{1,0:T(8,128)S(1)} %copy-done.5, ...), custom_call_target="tpu_custom_call" | custom-call | tf_op jit(solution)/shard_map/long_scan/pallas_call | solution.py:511
  49.5 1.5 %convert_element_type.3 = f32[64,8192]{1,0:T(8,128)} convert(bf16[64,8192]{1,0:T(8,128)(2,1)S(1)} %long_scan.1) | non-fusion elementwise | flops 524288 | bytes 3145728 | tf_op jit(solution)/shard_map/convert_element_type | solution.py:573
Async XLA Ops:
  0.0 0.9 %copy-start = (bf16[128,512]{1,0:T(8,128)(2,1)S(1)}, bf16[128,512]{1,0:T(8,128)(2,1)}, u32[]{:S(2)}) copy-start(bf16[128,512]{1,0:T(8,128)(2,1)} %query_hbm.1) | copy-start | bytes 393220
  0.9 0.9 %copy-start.1 = (bf16[128,512]{1,0:T(8,128)(2,1)S(1)}, bf16[128,512]{1,0:T(8,128)(2,1)}, u32[]{:S(2)}) copy-start(bf16[128,512]{1,0:T(8,128)(2,1)} %key_hbm.1) | copy-start | bytes 393220
  1.8 0.9 %copy-start.2 = (bf16[128,512]{1,0:T(8,128)(2,1)S(1)}, bf16[128,512]{1,0:T(8,128)(2,1)}, u32[]{:S(2)}) copy-start(bf16[128,512]{1,0:T(8,128)(2,1)} %value_hbm.1) | copy-start | bytes 393220
  2.7 0.8 %copy-start.3 = (f32[3,7,512]{2,1,0:T(8,128)S(1)}, f32[3,7,512]{2,1,0:T(8,128)}, u32[]{:S(2)}) copy-start(f32[3,7,512]{2,1,0:T(8,128)} %short_ref.1) | copy-start | bytes 129028
  3.5 0.8 %copy-start.4 = (f32[16,512]{1,0:T(8,128)S(1)}, f32[16,512]{1,0:T(8,128)}, u32[]{:S(2)}) copy-start(f32[16,512]{1,0:T(8,128)} %residue_ref.1) | copy-start | bytes 98308
  4.3 0.8 %copy-start.5 = (f32[16,512]{1,0:T(8,128)S(1)}, f32[16,512]{1,0:T(8,128)}, u32[]{:S(2)}) copy-start(f32[16,512]{1,0:T(8,128)} %rate_ref.1) | copy-start | bytes 98308

commit v4 on v3

--- a/solution.py
+++ b/solution.py
@@ -47,6 +47,7 @@
     driven,
     local_states,
     entry_states,
+    first_state,
     state_rows,
     powers,
     response,
@@ -243,11 +244,7 @@
     for copy in cross_copies[:2]:
         copy.start()
     weight_copy.start()
-    for copy in tail_copies:
-        copy.wait_recv()
     for at in range(3):
-        last = tails[at].astype(jnp.float32)[TAIL - BLOCK :]
-        ext[at, 0:BLOCK] = jnp.where(me == 0, 0.0, last)
         ext[at, BLOCK:] = raw[at].astype(jnp.float32)
 
     def short_rows(at, filter_at, start):
@@ -257,12 +254,11 @@
             total = total + short_ref[filter_at, j : j + 1, :] * window[BLOCK - j : 3 * BLOCK - j]
         return total
 
-    @pl.loop(0, tokens // (2 * BLOCK))
-    def _(i):
+    def drive(i):
         start = pl.multiple_of(i * (2 * BLOCK), 2 * BLOCK)
         driven[pl.ds(start, 2 * BLOCK)] = short_rows(0, 1, start) * short_rows(1, 2, start)
 
-    for part in range(2):
+    def scan_blocks(first, last, part):
         columns = slice(part * half, (part + 1) * half)
 
         def advance(b, state):
@@ -273,7 +269,22 @@
                 state = state + powers[BLOCK - 1 - j, part] * rows[j : j + 1, :]
             return state
 
-        own_total[part] = lax.fori_loop(0, blocks, advance, jnp.zeros((order, half), jnp.float32))
+        return lax.fori_loop(first, last, advance, jnp.zeros((order, half), jnp.float32))
+
+    pl.loop(1, tokens // (2 * BLOCK))(drive)
+    later = [scan_blocks(2, blocks, part) for part in range(2)]
+    for copy in tail_copies:
+        copy.wait_recv()
+    for at in range(3):
+        last = tails[at].astype(jnp.float32)[TAIL - BLOCK :]
+        ext[at, 0:BLOCK] = jnp.where(me == 0, 0.0, last)
+    pl.loop(0, 1)(drive)
+    for part in range(2):
+        columns = slice(part * half, (part + 1) * half)
+        state = scan_blocks(0, 2, part)
+        first_state[part] = state
+        decay = jnp.exp(-(rate_ref[:, columns] * float(tokens - 2 * BLOCK)))
+        own_total[part] = later[part] + state * decay
 
     pair_copy = pltpu.make_async_remote_copy(
         src_ref=own_total,
@@ -385,7 +396,10 @@
         for part in range(2):
             columns = slice(part * half, (part + 1) * half)
             decay = jnp.exp(-(rate_ref[:, columns] * float(out_rows)))
-            entry_states[part] = jnp.where(which == 0, entries[part], entries[part] * decay)
+            shift = jnp.exp(-(rate_ref[:, columns] * float(out_rows - 2 * BLOCK)))
+            entry_states[part] = jnp.where(
+                which == 0, entries[part], entries[part] * decay + first_state[part] * shift
+            )
 
         @pl.loop(0, steps)
         def _(step):
@@ -396,7 +410,10 @@
                 outs = []
                 for sub in range(2):
                     entry = entry_states[part]
-                    entry_states[part] = entry * powers[BLOCK, part]
+                    following = entry * powers[BLOCK, part]
+                    if sub == 1:
+                        following = following + jnp.where(i == 0, first_state[part], 0.0)
+                    entry_states[part] = following
                     state = local_states[2 * i + sub, part] + entry
                     rows = driven[pl.ds(pl.multiple_of(start + sub * BLOCK, BLOCK), BLOCK), columns]
                     out = taps[0, part] * rows
@@ -526,6 +543,7 @@
             pltpu.VMEM((tokens, width), jnp.bfloat16),
             pltpu.VMEM((tokens, width), f32),
             pltpu.VMEM((tokens // BLOCK, 2, order, half), f32),
+            pltpu.VMEM((2, order, half), f32),
             pltpu.VMEM((2, order, half), f32),
             pltpu.VMEM((2, order, half), f32),
             pltpu.VMEM((BLOCK + 1, 2, order, half), f32),
@@ -567,9 +585,8 @@
 
 
 def per_device(query_input, key_input, value_input, short_kernel, residues, rates, out_weight):
-    mixed = scan_call(
-        query_input, key_input, value_input, short_kernel, residues, rates, out_weight
-    )
+    arguments = (query_input, key_input, value_input, short_kernel, residues, rates, out_weight)
+    mixed = scan_call(*[pltpu.with_memory_space_constraint(a, pltpu.HBM) for a in arguments])
     return mixed.astype(jnp.float32)
 
 

time: 51.3 us -> 46.2 us (0.901)
  local copies, waits for them, and re-layouts: 5.02 us -> 0 us
    unnamed x12 -> x0, local copies, waits for them, and re-layouts: 5.02 us -> none
where the time goes in v4:
time: 46.2 us; the launch traced here: 46.1 us
  Pallas kernels  44.6 us (97%)
  other arithmetic  1.46 us (3%)
    pallas_call x1, Pallas kernels, scan_call(): pl.pallas_call(scan_kernel, out_shape=jax.ShapeDtypeStruct((out_rows, col...  44.6 us
    convert_element_type x1, other arithmetic, per_device(): return mixed.astype(jnp.float32)  1.46 us

profile of v4, /device:TPU:1, one launch (start us, length us, event | category | flops | bytes accessed | tf_op | source)
XLA Modules:
  0.0 46.1 jit_solution(18353904595997932457)
XLA Ops:
  0.0 44.6 %long_scan.1 = bf16[64,8192]{1,0:T(8,128)(2,1)S(1)} custom-call(bf16[128,512]{1,0:T(8,128)(2,1)} %query_hbm.1, bf16[128,512]{1,0:T(8,128)(2,1)} %key_hbm.1, bf16[128,512]{1,0:T(8,128)(2,1)} %value_hbm.1, f32[3,7,512]{2,1,0:T(8,128)} %short_ref.1, f32[16,512]{1,0:T(8,128)} %residue_ref.1, f32[16,512]{1,0:T(8,128)} %rate_ref.1, bf16[512,8192]{1,0:T(8,128)(2,1)} %weight_hbm.1), custom_call_target="tpu_custom_call" | custom-call | tf_op jit(solution)/shard_map/long_scan/pallas_call | solution.py:528
  44.6 1.5 %convert_element_type.3 = f32[64,8192]{1,0:T(8,128)} convert(bf16[64,8192]{1,0:T(8,128)(2,1)S(1)} %long_scan.1) | non-fusion elementwise | flops 524288 | bytes 3145728 | tf_op jit(solution)/shard_map/convert_element_type | solution.py:590

commit v5 on v4

--- a/solution.py
+++ b/solution.py
@@ -227,8 +227,6 @@
             response[r] = scale_row * jnp.exp(-(ages * rate_row))
 
     pl.semaphore_wait(barrier, len(peers))
-    for copy in loads:
-        copy.wait()
     tail_copies = []
     for at, source in enumerate((key_hbm, value_hbm, query_hbm)):
         copy = pltpu.make_async_remote_copy(
@@ -244,6 +242,8 @@
     for copy in cross_copies[:2]:
         copy.start()
     weight_copy.start()
+    for copy in loads:
+        copy.wait()
     for at in range(3):
         ext[at, BLOCK:] = raw[at].astype(jnp.float32)
 
@@ -467,8 +467,6 @@
         for at in range(len(CHUNKS)):
             if (direction, at) not in arrived:
                 spread_copies[direction, at].wait_recv()
-        second_copies[direction].wait_recv()
-    cross_copies[-1].wait_recv()
     rows_copies[2].wait_recv()
 
     def result_copy(n):
@@ -482,8 +480,7 @@
             device_id_type=MESH,
         )
 
-    @pl.loop(0, COLOURS)
-    def _(n):
+    def finish(n):
         column = pl.multiple_of(first_column + n * piece_columns, piece_columns)
         total = partial[n] + jnp.dot(
             rows_in[1], other_weight[n], preferred_element_type=jnp.float32
@@ -492,6 +489,18 @@
         to_sibling[n] = total[out_rows:]
         result_copy(n).start()
         out_ref[:, pl.ds(column, piece_columns)] = total[:out_rows]
+
+    @pl.loop(0, COLOURS - 2)
+    def _(k):
+        finish(shifted(k + (k >= 3).astype(jnp.int32) + (k >= 4).astype(jnp.int32)))
+
+    for direction in DIRECTIONS:
+        second_copies[direction].wait_recv()
+    cross_copies[-1].wait_recv()
+
+    @pl.loop(0, 2)
+    def _(k):
+        finish(shifted(3 + 2 * k))
 
     @pl.loop(0, COLOURS)
     def _(n):

time: 46.2 us -> 46.3 us (level)
  no operation moved by 1% of the time
where the time goes in v5:
time: 46.3 us; the launch traced here: 46.1 us
  Pallas kernels  44.7 us (97%)
  other arithmetic  1.46 us (3%)
    pallas_call x1, Pallas kernels, scan_call(): pl.pallas_call(scan_kernel, out_shape=jax.ShapeDtypeStruct((out_rows, col...  44.7 us
    convert_element_type x1, other arithmetic, per_device(): return mixed.astype(jnp.float32)  1.46 us

profile of v5, /device:TPU:1, one launch (start us, length us, event | category | flops | bytes accessed | tf_op | source)
XLA Modules:
  0.0 46.1 jit_solution(13668427717804233695)
XLA Ops:
  0.0 44.7 %long_scan.1 = bf16[64,8192]{1,0:T(8,128)(2,1)S(1)} custom-call(bf16[128,512]{1,0:T(8,128)(2,1)} %query_hbm.1, bf16[128,512]{1,0:T(8,128)(2,1)} %key_hbm.1, bf16[128,512]{1,0:T(8,128)(2,1)} %value_hbm.1, f32[3,7,512]{2,1,0:T(8,128)} %short_ref.1, f32[16,512]{1,0:T(8,128)} %residue_ref.1, f32[16,512]{1,0:T(8,128)} %rate_ref.1, bf16[512,8192]{1,0:T(8,128)(2,1)} %weight_hbm.1), custom_call_target="tpu_custom_call" | custom-call | tf_op jit(solution)/shard_map/long_scan/pallas_call | solution.py:537
  44.7 1.5 %convert_element_type.3 = f32[64,8192]{1,0:T(8,128)} convert(bf16[64,8192]{1,0:T(8,128)(2,1)S(1)} %long_scan.1) | non-fusion elementwise | flops 524288 | bytes 3145728 | tf_op jit(solution)/shard_map/convert_element_type | solution.py:599
